TPU v7x, 1024 devices: a whole 8x8x8 slice. The times are simulated.
1024 devices in a mesh: segment: 8 (over y), expert: 64 (over z, x), dp: 2 (over core).
Axes of the slice: x: 8, y: 8, z: 8, core: 2. Of those that a mesh axis runs over, the one named last changes fastest.
Arguments:
- activations: bfloat16 [8, 4096, 8, 512], P('segment', ('expert', 'dp')), may hold values from -6 to 6
- upstream: bfloat16 [8, 4096, 8, 512], P('segment', ('expert', 'dp')), may hold values from -6 to 6
- routes: int32 [8, 4096, 2], P('segment', ('expert', 'dp')), may hold values from 0 to 63, all different within a row; in each aligned block of 32 rows (0 to 31, 32 to 63, ..., all dimensions but the last counted through in order) at most 2 rows name the same one
- gate_codes: int32 [8, 4096, 2], P('segment', ('expert', 'dp')), may hold values from 1 to 32767
- weights: bfloat16 [8, 64, 9, 64, 512], P('segment', 'expert'), may hold values from -0.25 to 0.25
Outputs:
- input_grad: bfloat16 [8, 4096, 8, 512], P('segment', ('expert', 'dp'))
- weight_grad: float32 [8, 64, 9, 64, 512], P('segment', 'expert')
Inputs may be any that keep to these rules, and one draw needn't show every extreme that they name: `routes`: the two experts of a tile differ; the 32 tiles of one device name each expert at most 2 times, and on some devices one expert exactly 2 times.
All inputs are finite; a program needn't handle non-finite values.
Results may differ from a plain program's by a relative error of at most 0.004.
Values may be sent and summed in bfloat16 or wider, within the bound.
A program may use at most 64 MiB of HBM per device.

v0:
```python
import jax
import jax.numpy as jnp
import numpy as np
from jax import lax
from jax.sharding import PartitionSpec as P

TH = 4
TW = 2


def shifted(array, axis, by):
    count = lax.axis_size(axis)
    return lax.ppermute(array, axis, [(i, (i + by) % count) for i in range(count)])


def offsets_table():
    cell_count = TH * TW
    table = np.zeros((cell_count, cell_count, 9), np.float32)
    for source_cell in range(cell_count):
        for target_cell in range(cell_count):
            row_step = target_cell // TW - source_cell // TW
            col_step = target_cell % TW - source_cell % TW
            if abs(row_step) <= 1 and abs(col_step) <= 1:
                table[source_cell, target_cell, (row_step + 1) * 3 + col_step + 1] = 1.0
    return table


def by_group(rows, group_width):
    tile_count = rows.shape[0]
    cell_count = rows.shape[1]
    group_count = rows.shape[2] // group_width
    split = rows.reshape(tile_count, cell_count, group_count, group_width).transpose(2, 0, 1, 3)
    return split.reshape(group_count, tile_count, cell_count * group_width)


def transpose_conv(scaled_grads, weight):
    tile_count = scaled_grads.shape[0]
    cell_count = scaled_grads.shape[1]
    group_width = weight.shape[1]
    channels = weight.shape[2]
    group_count = channels // group_width
    selector = jnp.asarray(offsets_table(), jnp.bfloat16)
    split_weight = weight.reshape(9, group_width, group_count, group_width)
    blocks = jnp.einsum(
        "pqt,tcgo->gpoqc", selector, split_weight, preferred_element_type=jnp.float32
    )
    blocks = blocks.astype(jnp.bfloat16).reshape(
        group_count, cell_count * group_width, cell_count * group_width
    )
    grouped = by_group(scaled_grads, group_width)
    result = jnp.einsum("gnk,gkm->gnm", grouped, blocks, preferred_element_type=jnp.float32)
    result = result.reshape(group_count, tile_count, cell_count, group_width).transpose(1, 2, 0, 3)
    return result.reshape(tile_count, cell_count, channels)


def weight_corr(inputs, scaled_grads, group_width):
    cell_count = inputs.shape[1]
    channels = inputs.shape[2]
    group_count = channels // group_width
    grouped_inputs = by_group(inputs, group_width)
    grouped_grads = by_group(scaled_grads, group_width)
    moments = jnp.einsum(
        "gnk,gnm->gkm", grouped_inputs, grouped_grads, preferred_element_type=jnp.float32
    )
    moments = moments.reshape(group_count, cell_count, group_width, cell_count, group_width)
    selector = jnp.asarray(offsets_table(), jnp.float32)
    taps = jnp.einsum("gpcqo,qpt->tcgo", moments, selector, precision=lax.Precision.HIGHEST)
    return taps.reshape(9, group_width, channels)


def body(activations, upstream, routes, gate_codes, weights):
    incoming = shifted(upstream, "segment", -1)[0]
    inputs = activations[0]
    route_ids = routes[0]
    code_values = gate_codes[0].astype(jnp.float32)
    kernel = weights[0, 0]
    group_width = kernel.shape[1]
    per_device = inputs.shape[0]
    cell_count = inputs.shape[1]
    channels = inputs.shape[2]
    experts = lax.axis_size("expert")
    capacity = max(2, 4 * per_device // experts)
    gate_share = code_values / jnp.sum(code_values, axis=1, keepdims=True)
    scaled_grads = (gate_share[:, :, None, None] * incoming[:, None].astype(jnp.float32)).astype(
        jnp.bfloat16
    )
    grad_rows = scaled_grads.reshape(2 * per_device, cell_count * channels)
    input_rows = jnp.repeat(inputs, 2, axis=0).reshape(2 * per_device, cell_count * channels)
    flat_expert = route_ids.reshape(-1)
    matches = (flat_expert[:, None] == jnp.arange(experts, dtype=jnp.int32)[None, :]).astype(
        jnp.int32
    )
    earlier = jnp.cumsum(matches, axis=0) - matches
    slot_rank = jnp.sum(earlier * matches, axis=1)
    slot_place = flat_expert * capacity + slot_rank
    chooser = (
        slot_place[None, :] == jnp.arange(experts * capacity, dtype=jnp.int32)[:, None]
    ).astype(jnp.bfloat16)

    def pack_slots(rows):
        packed = jnp.dot(chooser, rows, preferred_element_type=jnp.float32).astype(jnp.bfloat16)
        return packed.reshape(experts, capacity, cell_count, channels)

    inputs_recv, grads_recv = (
        lax.all_to_all(pack_slots(input_rows), "expert", split_axis=0, concat_axis=0, tiled=True),
        lax.all_to_all(pack_slots(grad_rows), "expert", split_axis=0, concat_axis=0, tiled=True),
    )
    flat_grads = grads_recv.reshape(experts * capacity, cell_count, channels)
    answers = transpose_conv(flat_grads, kernel).astype(jnp.bfloat16)
    returned = lax.all_to_all(
        answers.reshape(experts, capacity, cell_count, channels),
        "expert",
        split_axis=0,
        concat_axis=0,
        tiled=True,
    )
    flat_inputs = inputs_recv.reshape(experts * capacity, cell_count, channels)
    local_grad = weight_corr(flat_inputs, flat_grads, group_width)
    flat_answers = returned.reshape(experts * capacity, cell_count * channels)
    per_route = jnp.dot(chooser.T, flat_answers, preferred_element_type=jnp.float32).reshape(
        per_device, 2, cell_count, channels
    )
    input_grad = (incoming.astype(jnp.float32) + per_route[:, 0] + per_route[:, 1]).astype(
        jnp.bfloat16
    )
    total_grad = lax.psum(local_grad, "dp") / per_device
    return (input_grad[None], total_grad[None, None])


def solution(mesh):
    placed = (
        P("segment", ("expert", "dp"), None, None),
        P("segment", ("expert", "dp"), None, None),
        P("segment", ("expert", "dp"), None),
        P("segment", ("expert", "dp"), None),
        P("segment", "expert", None, None, None),
    )
    return jax.shard_map(
        body,
        mesh=mesh,
        in_specs=placed,
        out_specs=(
            P("segment", ("expert", "dp"), None, None),
            P("segment", "expert", None, None, None),
        ),
        check_vma=False,
    )
```

profile of v0, /device:TPU:1, one launch (start us, length us, event | category | flops | bytes accessed | tf_op | source)
XLA Modules:
  0.0 226.6 jit_solution(12966285984184553543)
XLA Ops:
  7.2 0.8 copy.20
  7.9 0.1 reshape_squeeze.6
  8.1 0.1 reduce_window_sum.11
  8.2 0.2 select_reduce_fusion
  8.4 1.0 broadcast_in_dim.4
  9.4 0.2 copy.45
  9.6 0.4 convolution_convert_fusion
  10.0 1.4 copy.46
  11.4 23.2 %all-to-all-start.2 = ((bf16[64,2,8,512]{3,2,1,0:T(8,128)(2,1)}), bf16[64,2,8,512]{3,2,1,0:T(8,128)(2,1)S(1)}, u32[]{:S(2)}, u32[]{:S(2)}) async-start(bf16[64,2,8,512]{3,2,1,0:T(8,128)(2,1)} %bitcast.54), calls=%async_computation.2 | async-start | bytes 2097152 | tf_op jit(solution)/shard_map/all_to_all | solution.py:105
  34.6 0.1 copy.19
  34.7 5.9 %collective-permute-start = (bf16[1,32,8,512]{3,1,2,0:T(8,128)(2,1)S(1)}, bf16[1,32,8,512]{3,1,2,0:T(8,128)(2,1)S(1)}, u32[]{:S(2)}, u32[]{:S(2)}) collective-permute-start(bf16[1,32,8,512]{3,1,2,0:T(8,128)(2,1)S(1)} %copy.19), channel_id=1, source_target_pairs={{0,896},{128,0},{256,128},{384,256},{512,384},{640,512},{768,640},... | collective-permute-start | bytes 786440 | tf_op jit(solution)/shard_map/ppermute | solution.py:13
  40.6 0.1 copy.22
  40.7 0.1 convert_element_type.66
  40.9 0.1 div.21
  41.0 4.2 %collective-permute-done = bf16[1,32,8,512]{3,1,2,0:T(8,128)(2,1)S(1)} collective-permute-done((bf16[1,32,8,512]{3,1,2,0:T(8,128)(2,1)S(1)}, bf16[1,32,8,512]{3,1,2,0:T(8,128)(2,1)S(1)}, u32[]{:S(2)}, u32[]{:S(2)}) %collective-permute-start) | collective-permute-done | bytes 262176 | tf_op jit(solution)/shard_map/ppermute | solution.py:13
  45.3 0.3 copy.23
  45.6 0.1 mul.44
  45.7 0.6 copy.42
  46.3 0.5 convolution_convert_fusion.1
  46.8 1.4 copy.43
  48.2 13.8 %all-to-all-done.2 = bf16[64,2,8,512]{3,2,1,0:T(8,128)(2,1)S(1)} async-done(((bf16[64,2,8,512]{3,2,1,0:T(8,128)(2,1)}), bf16[64,2,8,512]{3,2,1,0:T(8,128)(2,1)S(1)}, u32[]{:S(2)}, u32[]{:S(2)}) %all-to-all-start.2) | async-done | bytes 1048608 | tf_op jit(solution)/shard_map/all_to_all | solution.py:105
  62.0 8.2 %all-to-all-start = ((bf16[64,2,8,512]{3,2,1,0:T(8,128)(2,1)}), bf16[64,2,8,512]{3,2,1,0:T(8,128)(2,1)}, u32[]{:S(2)}, u32[]{:S(2)}) async-start(bf16[64,2,8,512]{3,2,1,0:T(8,128)(2,1)} %bitcast.41), calls=%async_computation | async-start | bytes 2097152 | tf_op jit(solution)/shard_map/all_to_all | solution.py:106
  70.2 0.6 reshape_squeeze.7
  70.8 5.5 %convert_bitcast_fusion = bf16[8,8,64,8,64]{2,3,0,4,1:T(8,128)(2,1)} fusion(bf16[8,8,9,1,1]{2,1,4,3,0:T(8,128)(2,1)S(1)} %copy-done.6, bf16[9,64,8,64]{3,2,1,0:T(8,128)(2,1)S(1)} %reshape_squeeze.7), kind=kOutput, calls=%fused_computation | convolution fusion | flops 39845888 | bytes 4785280 | tf_op jit(solution)/shard_map/pqt,tcgo->gpoqc/dot_general | solution.py:44
  76.3 15.0 %copy.26 = bf16[8,8,64,8,64]{4,3,2,1,0:T(8,128)(2,1)} copy(bf16[8,8,64,8,64]{2,3,0,4,1:T(8,128)(2,1)} %convert_bitcast_fusion) | data formatting | bytes 8388608 | tf_op jit(solution)/shard_map/convert_element_type | solution.py:47
  91.3 11.8 %reshape.104 = bf16[8,512,512]{2,1,0:T(8,128)(2,1)} reshape(bf16[8,8,64,8,64]{4,3,2,1,0:T(8,128)(2,1)} %copy.26) | data formatting | bytes 8388608 | tf_op jit(solution)/shard_map/reshape | solution.py:47
  103.2 1.1 reshape_reshape.12
  104.3 2.9 %copy.31 = bf16[8,128,8,64]{1,3,2,0:T(8,128)(2,1)} copy(bf16[8,128,8,64]{3,0,2,1:T(8,128)(2,1)S(1)} %bitcast.91) | data formatting | bytes 2097152 | tf_op jit(solution)/shard_map/transpose | solution.py:32
  107.2 2.8 %reshape_reshape.10 = bf16[128,8,8,64]{3,2,1,0:T(8,128)(2,1)S(1)} reshape(bf16[64,2,8,512]{3,2,1,0:T(8,128)(2,1)} %all-to-all-done) | data formatting | bytes 2097152 | tf_op jit(solution)/shard_map/reshape;reshape | solution.py:32
  110.0 2.1 copy.24
  112.1 3.0 %convolution_convert_fusion.2 = bf16[8,128,512]{2,1,0:T(8,128)(2,1)S(1)} fusion(bf16[8,128,512]{1,2,0:T(8,128)(2,1)S(1)} %bitcast.89, bf16[8,512,512]{2,1,0:T(8,128)(2,1)} %reshape.104), kind=kOutput, calls=%fused_computation.6 | convolution fusion | flops 537395200 | bytes 6291456 | tf_op jit(solution)/shard_map/gnk,gkm->gnm/dot_general | solution.py:51
  115.1 1.3 copy.28
  116.4 3.9 %copy.29 = bf16[128,8,8,64]{3,2,1,0:T(8,128)(2,1)S(1)} copy(bf16[128,8,8,64]{0,3,1,2:T(8,128)(2,1)} %bitcast.94) | data formatting | bytes 2097152 | tf_op jit(solution)/shard_map/convert_element_type | solution.py:109
  120.3 2.1 convert_element_type.76
  122.4 12.0 %all-to-all-start.1 = ((bf16[64,2,8,512]{3,2,1,0:T(8,128)(2,1)}), bf16[64,2,8,512]{3,2,1,0:T(8,128)(2,1)S(1)}, u32[]{:S(2)}, u32[]{:S(2)}) async-start(bf16[64,2,8,512]{3,2,1,0:T(8,128)(2,1)} %convert_element_type.76), calls=%async_computation.1 | async-start | bytes 2097152 | tf_op jit(solution)/shard_map/all_to_all | solution.py:110
  134.5 4.5 %fusion.13 = f32[8,512,512]{2,1,0:T(8,128)} fusion(bf16[8,128,512]{1,2,0:T(8,128)(2,1)S(1)} %bitcast.93, bf16[8,128,512]{1,2,0:T(8,128)(2,1)S(1)} %bitcast.90), kind=kOutput, calls=%fused_computation.30 | convolution fusion | flops 536870912 | bytes 10485760 | tf_op jit(solution)/shard_map/gnk,gnm->gkm/dot_general | solution.py:62
  139.0 12.9 %reshape.108 = f32[8,8,64,8,64]{4,3,2,1,0:T(8,128)} reshape(f32[8,512,512]{2,1,0:T(8,128)} %fusion.13) | data formatting | bytes 16777216 | tf_op jit(solution)/shard_map/reshape | solution.py:65
  151.9 11.4 %convolution_bitcast_fusion = f32[9,64,8,64]{3,0,1,2:T(8,128)S(1)} fusion(f32[8,8,64,8,64]{4,3,2,1,0:T(8,128)} %reshape.108, f32[8,8,9,1,1]{2,0,1,4,3:T(8,128)S(1)} %copy-done.5), kind=kOutput, calls=%fused_computation.3 | convolution fusion | flops 226492416 | bytes 9570560 | tf_op jit(solution)/shard_map/gpcqo,qpt->tcgo/dot_general | solution.py:67
  163.3 1.4 copy.34
  164.7 1.6 reshape.109
  166.3 0.1 reduce_sum.21
  166.5 48.3 %all-reduce.2.cloned.1.call-done = f32[9,64,512]{2,1,0:T(8,128)} async-done(((f32[9,64,512]{2,1,0:T(8,128)}), f32[9,64,512]{2,1,0:T(8,128)}) %all-reduce.2.cloned.1.call-update) | async-done | bytes 1179664 | tf_op jit(solution)/shard_map/psum | solution.py:126
  214.7 2.4 %multiply_bitcast_fusion = f32[1,1,9,64,512]{4,3,2,1,0:T(8,128)} fusion(f32[9,64,512]{2,1,0:T(8,128)} %all-reduce.2.cloned.1.call-done), kind=kLoop, calls=%fused_computation.7 | loop fusion | flops 294912 | bytes 2359296 | tf_op jit(solution)/shard_map/broadcast_in_dim | solution.py:127
  217.2 0.4 copy.44
  217.6 0.7 copy.30
  218.2 0.5 fusion.10
  218.8 0.1 fusion.3
  218.9 0.9 copy.35
  (31 shorter events, 0.4 us)
Async XLA Ops:
  10.0 24.5 %copy-start.4 = (bf16[1,32,8,512]{3,2,1,0:T(8,128)(2,1)S(1)}, bf16[1,32,8,512]{3,2,1,0:T(8,128)(2,1)}, u32[]{:S(2)}) copy-start(bf16[1,32,8,512]{3,2,1,0:T(8,128)(2,1)} %param.8) | copy-start | bytes 786436
  10.0 30.5 %copy-start.8 = (s32[1,32,2]{1,2,0:T(2,128)S(1)}, s32[1,32,2]{1,2,0:T(2,128)}, u32[]{:S(2)}) copy-start(s32[1,32,2]{1,2,0:T(2,128)} %param.10) | copy-start | bytes 772
  11.4 50.6 %all-to-all-start.2 = ((bf16[64,2,8,512]{3,2,1,0:T(8,128)(2,1)}), bf16[64,2,8,512]{3,2,1,0:T(8,128)(2,1)S(1)}, u32[]{:S(2)}, u32[]{:S(2)}) async-start(bf16[64,2,8,512]{3,2,1,0:T(8,128)(2,1)} %bitcast.54), calls=%async_computation.2 | async-start | bytes 2097152 | tf_op jit(solution)/shard_map/all_to_all | solution.py:105
  34.7 10.5 %collective-permute-start = (bf16[1,32,8,512]{3,1,2,0:T(8,128)(2,1)S(1)}, bf16[1,32,8,512]{3,1,2,0:T(8,128)(2,1)S(1)}, u32[]{:S(2)}, u32[]{:S(2)}) collective-permute-start(bf16[1,32,8,512]{3,1,2,0:T(8,128)(2,1)S(1)} %copy.19), channel_id=1, source_target_pairs={{0,896},{128,0},{256,128},{384,256},{512,384},{640,512},{768,640},... | collective-permute-start | bytes 786440 | tf_op jit(solution)/shard_map/ppermute | solution.py:13
  45.2 1.1 copy-start.1
  46.8 23.3 %copy-start.3 = (bf16[1,1,9,64,512]{4,3,2,1,0:T(8,128)(2,1)S(1)}, bf16[1,1,9,64,512]{4,3,2,1,0:T(8,128)(2,1)}, u32[]{:S(2)}) copy-start(bf16[1,1,9,64,512]{4,3,2,1,0:T(8,128)(2,1)} %param.11) | copy-start | bytes 1769476
  48.2 22.6 %copy-start.6 = (bf16[8,8,9,1,1]{2,1,4,3,0:T(8,128)(2,1)S(1)}, bf16[8,8,9,1,1]{2,1,4,3,0:T(8,128)(2,1)}, u32[]{:S(2)}) copy-start(bf16[8,8,9,1,1]{2,1,4,3,0:T(8,128)(2,1)} %constant.24) | copy-start | bytes 3460
  62.0 45.2 %all-to-all-start = ((bf16[64,2,8,512]{3,2,1,0:T(8,128)(2,1)}), bf16[64,2,8,512]{3,2,1,0:T(8,128)(2,1)}, u32[]{:S(2)}, u32[]{:S(2)}) async-start(bf16[64,2,8,512]{3,2,1,0:T(8,128)(2,1)} %bitcast.41), calls=%async_computation | async-start | bytes 2097152 | tf_op jit(solution)/shard_map/all_to_all | solution.py:106
  122.4 12.1 %copy-start = (bf16[8,128,8,64]{1,3,2,0:T(8,128)(2,1)S(1)}, bf16[8,128,8,64]{1,3,2,0:T(8,128)(2,1)}, u32[]{:S(2)}) copy-start(bf16[8,128,8,64]{1,3,2,0:T(8,128)(2,1)} %copy.31) | copy-start | bytes 3145732
  122.4 94.7 %all-to-all-start.1 = ((bf16[64,2,8,512]{3,2,1,0:T(8,128)(2,1)}), bf16[64,2,8,512]{3,2,1,0:T(8,128)(2,1)S(1)}, u32[]{:S(2)}, u32[]{:S(2)}) async-start(bf16[64,2,8,512]{3,2,1,0:T(8,128)(2,1)} %convert_element_type.76), calls=%async_computation.1 | async-start | bytes 2097152 | tf_op jit(solution)/shard_map/all_to_all | solution.py:110
  134.5 80.3 %all-reduce.2.cloned.1.call-start = ((), (), s32[]{:S(2)}) async-start(), calls=%async_computation.3 | async-start | bytes 2359296 | tf_op jit(solution)/shard_map/psum | solution.py:126
  139.0 12.9 %copy-start.5 = (f32[8,8,9,1,1]{2,0,1,4,3:T(8,128)S(1)}, f32[8,8,9,1,1]{2,0,1,4,3:T(8,128)}, u32[]{:S(2)}) copy-start(f32[8,8,9,1,1]{2,0,1,4,3:T(8,128)} %constant.25) | copy-start | bytes 6916
  164.7 1.8 copy-start.7
  217.6 1.2 copy-start.2
Sparse Core Ops, SparseCore 0:
  166.4 48.2 all-reduce.1
where the time goes:
time: 228 us; the launch traced here: 227 us
  local copies, waits for them, and re-layouts  67.9 us (30%)
  waiting for transfers between devices  66.3 us (29%)
  starting transfers between devices  49.3 us (22%)
  matrix products  25.8 us (11%)
  between operations  14.4 us (6%)
  other arithmetic  3.01 us (1%)
    psum x1, waiting for transfers between devices, body(): total_grad = lax.psum(local_grad, 'dp') / per_device  48.3 us
    all_to_all x1, starting transfers between devices, body(): lax.all_to_all(pack_slots(input_rows), 'expert', split_axis=0, concat_axi...  23.2 us
    convert_element_type x1, local copies, waits for them, and re-layouts, transpose_conv(): blocks.astype(jnp.bfloat16)  15 us
    all_to_all x1, waiting for transfers between devices, body(): lax.all_to_all(pack_slots(input_rows), 'expert', split_axis=0, concat_axi...  13.8 us
    reshape x1, local copies, waits for them, and re-layouts, weight_corr(): moments.reshape(group_count, cell_count, group_width, cell_count, group_w...  12.9 us
    all_to_all x1, starting transfers between devices, body(): lax.all_to_all(answers.reshape(experts, capacity, cell_count, channels),...  12 us
    reshape x1, local copies, waits for them, and re-layouts, transpose_conv(): blocks.astype(jnp.bfloat16)  11.8 us
    dot_general x1, matrix products, weight_corr(): jnp.einsum('gpcqo,qpt->tcgo', moments, selector, precision=lax.Precision....  11.4 us
  transfers between devices with their start and end apart: 5, of which 3 were waited for; matrix products, arithmetic and copies ran while one was open for 33% of the time, Pallas kernels for 0%

commit v1 on v0

v1 whole, which is shorter than its diff:
```python
import functools
import math

import jax
import jax.numpy as jnp
from jax import lax
from jax.experimental import pallas as pl
from jax.experimental.pallas import tpu as pltpu
from jax.sharding import PartitionSpec as P

TH = 4
TW = 2
CELLS = TH * TW
CAP = 2
ROWS = CAP * CELLS
HALF = 256
TAPS = [(a, b) for a in (-1, 0, 1) for b in (-1, 0, 1)]
MESH = pl.DeviceIdType.MESH
NT = (((1,), (1,)), ((), ()))


def dot(a, b):
    return jnp.dot(a, b, preferred_element_type=jnp.float32)


def dot_nt(a, b):
    return lax.dot_general(a, b, NT, preferred_element_type=jnp.float32)


def iota(shape, axis):
    return lax.broadcasted_iota(jnp.int32, shape, axis)


def kernel(
    side, segments,
    routes_ref, codes_ref, x_ref, up_ref, w_ref,
    dx_ref, dw_ref,
    px, pd, an, xr, dr, ar, dy, choose, chooset, gates, dall, bd, xt, acc, dwm, dwo,
    send_sem, relay_sem, x_sem, d_sem, a_sem, dw_send, dw_sem,
):
    experts = side * side
    tiles = routes_ref.shape[1]
    channels = x_ref.shape[1]
    halves = channels // HALF
    gw = w_ref.shape[1]
    groups = HALF // gw
    block = side * ROWS

    seg = lax.axis_index("segment")
    me = lax.axis_index("expert")
    rep = lax.axis_index("dp")
    my_z, my_x = me // side, me % side

    def offsets(o):
        step_x = o % side
        return (o // side + step_x) % side, step_x

    def ahead(o):
        step_z, step_x = offsets(o)
        return ((my_z + step_z) % side) * side + (my_x + step_x) % side

    def behind(o):
        step_z, step_x = offsets(o)
        return ((my_z + side - step_z) % side) * side + (my_x + side - step_x) % side

    barrier = pltpu.get_barrier_semaphore()

    def greet(o, carry):
        pl.semaphore_signal(barrier, inc=1, device_id={"expert": ahead(o)}, device_id_type=MESH)
        return carry

    seg_before = (seg + segments - 1) % segments
    seg_after = (seg + 1) % segments
    pl.semaphore_signal(barrier, inc=1, device_id={"segment": seg_before}, device_id_type=MESH)
    pl.semaphore_signal(barrier, inc=1, device_id={"segment": seg_after}, device_id_type=MESH)
    pl.semaphore_signal(barrier, inc=1, device_id={"dp": 1 - rep}, device_id_type=MESH)
    lax.fori_loop(1, experts, greet, 0)

    first = routes_ref[0:1, :]
    second = routes_ref[1:2, :]
    codes = codes_ref[...].astype(jnp.float32)
    total = codes[0:1, :] + codes[1:2, :]
    gate_first = codes[0:1, :] / total
    gate_second = codes[1:2, :] / total
    earlier = (iota((tiles, tiles), 0) < iota((tiles, tiles), 1)).astype(jnp.bfloat16)
    spread = (iota((tiles, tiles * CELLS), 1) // CELLS == iota((tiles, tiles * CELLS), 0)).astype(
        jnp.bfloat16
    )
    same_cell = (
        iota((block, tiles * CELLS), 0) % CELLS == iota((block, tiles * CELLS), 1) % CELLS
    )

    def pack_x(k, carry):
        row = iota((block, tiles), 0)
        step_x = row // ROWS
        step_z = (step_x + k) % side
        expert = ((my_z + step_z) % side) * side + (my_x + step_x) % side
        slot = (row // CELLS) % CAP
        is_first = first == expert
        named = is_first | (second == expert)
        rank = dot(named.astype(jnp.float32).astype(jnp.bfloat16), earlier)
        taken = jnp.where(named & (rank == slot.astype(jnp.float32)), 1.0, 0.0)
        gate = jnp.sum(taken * jnp.where(is_first, gate_first, gate_second), axis=1, keepdims=True)
        rows = pl.ds(pl.multiple_of(k * block, block), block)
        gates[rows, :] = gate
        chosen = jnp.where(same_cell, dot(taken.astype(jnp.bfloat16), spread), 0.0).astype(
            jnp.bfloat16
        )
        choose[rows, :] = chosen
        packed = dot(chosen, x_ref[...]).astype(jnp.bfloat16)
        px[pl.ds(k * side, side)] = packed.reshape(side, ROWS, channels)
        return carry

    lax.fori_loop(0, side, pack_x, 0)

    pl.semaphore_wait(barrier, experts + 2)

    relay = pltpu.make_async_remote_copy(
        src_ref=up_ref, dst_ref=dy, send_sem=relay_sem.at[0], recv_sem=relay_sem.at[1],
        device_id={"segment": seg_before}, device_id_type=MESH,
    )
    relay.start()

    def send(source, target, o, kind, sem, device):
        pltpu.make_async_remote_copy(
            src_ref=source.at[o], dst_ref=target.at[o],
            send_sem=send_sem.at[kind], recv_sem=sem.at[o // side],
            device_id={"expert": device}, device_id_type=MESH,
        ).start()

    def keep(source, target, sem):
        pltpu.make_async_copy(source.at[0], target.at[0], sem.at[0]).start()

    def send_x(o, carry):
        send(px, xr, o, 0, x_sem, ahead(o))
        return carry

    keep(px, xr, x_sem)
    lax.fori_loop(1, experts, send_x, 0)

    same_group = iota((HALF, HALF), 0) // gw == iota((HALF, HALF), 1) // gw
    for half in range(halves):
        for tap in range(9):
            piece = w_ref[tap, :, half * HALF:(half + 1) * HALF]
            piled = jnp.concatenate([piece] * groups, axis=0)
            bd[half, :, tap * HALF:(tap + 1) * HALF] = jnp.where(
                same_group, piled, jnp.zeros_like(piled)
            )

    relay.wait_recv()

    def pack_d(k, carry):
        rows = pl.ds(pl.multiple_of(k * block, block), block)
        packed = (dot(choose[rows, :], dy[...]) * gates[rows, :]).astype(jnp.bfloat16)
        pd[pl.ds(k * side, side)] = packed.reshape(side, ROWS, channels)
        return carry

    lax.fori_loop(0, side, pack_d, 0)

    def send_d(o, carry):
        send(pd, dr, o, 1, d_sem, ahead(o))
        return carry

    keep(pd, dr, d_sem)
    lax.fori_loop(1, experts, send_d, 0)

    eye = (
        iota((tiles * CELLS, tiles * CELLS), 0) == iota((tiles * CELLS, tiles * CELLS), 1)
    ).astype(jnp.bfloat16)
    chooset[...] = dot_nt(eye, choose[...]).astype(jnp.bfloat16)

    def arrived(target, k, sem):
        part = target.at[pl.ds(k * side, side)]
        pltpu.make_async_copy(part, part, sem.at[k]).wait()

    tiles_here = side * CAP
    cell = iota((tiles_here, CELLS, HALF), 1)
    cell_i, cell_j = cell // TW, cell % TW

    def answer(k, carry):
        arrived(dr, k, d_sem)
        rows = pl.ds(pl.multiple_of(k * block, block), block)
        grads = dr[pl.ds(k * side, side)].reshape(block, channels)
        for half in range(halves):
            part = grads[:, half * HALF:(half + 1) * HALF]
            wide = part.astype(jnp.float32).reshape(tiles_here, CELLS, HALF)
            for tap, (a, b) in enumerate(TAPS):
                if a == 0 and b == 0:
                    moved = part
                else:
                    rolled = pltpu.roll(wide, (a * TW + b) % CELLS, 1)
                    valid = (
                        (cell_i - a >= 0) & (cell_i - a < TH) & (cell_j - b >= 0) & (cell_j - b < TW)
                    )
                    moved = jnp.where(valid, rolled, 0.0).reshape(block, HALF).astype(jnp.bfloat16)
                dall[half, rows, tap * HALF:(tap + 1) * HALF] = moved
            result = dot_nt(dall[half, rows, :], bd[half]).astype(jnp.bfloat16)
            an[pl.ds(k * side, side), :, half * HALF:(half + 1) * HALF] = result.reshape(
                side, ROWS, HALF
            )

        def send_a(j, inner):
            o = k * side + j

            @pl.when(o > 0)
            def _():
                send(an, ar, o, 2, a_sem, behind(o))

            @pl.when(o == 0)
            def _():
                keep(an, ar, a_sem)

            return inner

        lax.fori_loop(0, side, send_a, 0)
        return carry

    lax.fori_loop(0, side, answer, 0)

    all_x = xr.at[...]
    for k in range(side):
        arrived(xr, k, x_sem)
    eye_half = (iota((HALF, HALF), 0) == iota((HALF, HALF), 1)).astype(jnp.bfloat16)
    for half in range(halves):
        part = all_x[:, :, half * HALF:(half + 1) * HALF].reshape(experts * ROWS, HALF)
        xt[half] = dot_nt(eye_half, part).astype(jnp.bfloat16)

    lane_group = iota((gw, HALF), 1) // gw

    def swap(tap):
        return pltpu.make_async_remote_copy(
            src_ref=dwm.at[tap], dst_ref=dwo.at[tap],
            send_sem=dw_send.at[tap], recv_sem=dw_sem.at[tap],
            device_id={"dp": 1 - rep}, device_id_type=MESH,
        )

    for tap in range(9):
        for half in range(halves):
            full = dot(xt[half], dall[half, :, tap * HALF:(tap + 1) * HALF])
            picked = jnp.zeros((gw, HALF), jnp.float32)
            for g in range(groups):
                picked = jnp.where(lane_group == g, full[g * gw:(g + 1) * gw, :], picked)
            dwm[tap, :, half * HALF:(half + 1) * HALF] = picked
        swap(tap).start()

    acc[...] = dy[...].astype(jnp.float32)

    def combine(k, carry):
        arrived(ar, k, a_sem)
        rows = ar[pl.ds(k * side, side)].reshape(block, channels)
        cols = pl.ds(pl.multiple_of(k * block, block), block)
        acc[...] += dot(chooset[:, cols], rows)
        return carry

    lax.fori_loop(0, side, combine, 0)
    dx_ref[...] = acc[...].astype(jnp.bfloat16)

    for tap in range(9):
        swap(tap).wait_recv()
        dw_ref[tap] = (dwm[tap] + dwo[tap]) * (1.0 / tiles)

    relay.wait_send()
    for tap in range(9):
        swap(tap).wait_send()
    for kind, source in enumerate((px, pd, an)):
        sent = source.at[pl.ds(1, experts - 1)]
        pltpu.make_async_copy(sent, sent, send_sem.at[kind]).wait()


def body(side, segments, activations, upstream, routes, gate_codes, weights):
    _, tiles, cells, channels = activations.shape
    taps, gw = weights.shape[2], weights.shape[3]
    experts = side * side
    message = (experts, ROWS, channels)
    halves = channels // HALF
    vmem = pl.BlockSpec(memory_space=pltpu.VMEM)
    bf16, f32 = jnp.bfloat16, jnp.float32
    dma = pltpu.SemaphoreType.DMA
    input_grad, weight_grad = pl.pallas_call(
        functools.partial(kernel, side, segments),
        out_shape=(
            jax.ShapeDtypeStruct((tiles * cells, channels), bf16),
            jax.ShapeDtypeStruct((taps, gw, channels), f32),
        ),
        in_specs=[vmem] * 5,
        out_specs=(vmem, vmem),
        scratch_shapes=[pltpu.VMEM(message, bf16)] * 6
        + [
            pltpu.VMEM((tiles * cells, channels), bf16),
            pltpu.VMEM((experts * ROWS, tiles * cells), bf16),
            pltpu.VMEM((tiles * cells, experts * ROWS), bf16),
            pltpu.VMEM((experts * ROWS, 1), f32),
            pltpu.VMEM((halves, experts * ROWS, 9 * HALF), bf16),
            pltpu.VMEM((halves, HALF, 9 * HALF), bf16),
            pltpu.VMEM((halves, HALF, experts * ROWS), bf16),
            pltpu.VMEM((tiles * cells, channels), f32),
            pltpu.VMEM((taps, gw, channels), f32),
            pltpu.VMEM((taps, gw, channels), f32),
            dma((3,)), dma((2,)), dma((side,)), dma((side,)), dma((side,)), dma((9,)), dma((9,)),
        ],
        compiler_params=pltpu.CompilerParams(
            collective_id=0, has_side_effects=True, vmem_limit_bytes=56 * 1024 * 1024
        ),
    )(
        routes[0].T,
        gate_codes[0].T,
        activations.reshape(tiles * cells, channels),
        upstream.reshape(tiles * cells, channels),
        weights[0, 0],
    )
    return (
        input_grad.reshape(1, tiles, cells, channels),
        weight_grad.reshape(1, 1, taps, gw, channels),
    )


def solution(mesh):
    side = math.isqrt(mesh.shape["expert"])
    placed = (
        P("segment", ("expert", "dp"), None, None),
        P("segment", ("expert", "dp"), None, None),
        P("segment", ("expert", "dp"), None),
        P("segment", ("expert", "dp"), None),
        P("segment", "expert", None, None, None),
    )
    return jax.shard_map(
        functools.partial(body, side, mesh.shape["segment"]),
        mesh=mesh,
        in_specs=placed,
        out_specs=(
            P("segment", ("expert", "dp"), None, None),
            P("segment", "expert", None, None, None),
        ),
        check_vma=False,
    )
```

time: 228 us -> 106 us (0.46)
  the two profiles are of different devices: /device:TPU:1 before, /device:TPU:44 now
where the time goes in v1:
time: 106 us; the launch traced here: 105 us
  Pallas kernels  101 us (95%)
  local copies, waits for them, and re-layouts  4.03 us (4%)
    pallas_call x1, Pallas kernels, body(): pl.pallas_call(functools.partial(kernel, side, segments), out_shape=(jax....  101 us
    unnamed x2, local copies, waits for them, and re-layouts  4.03 us

profile of v1, /device:TPU:44, one launch (start us, length us, event | category | flops | bytes accessed | tf_op | source)
XLA Modules:
  0.0 105.5 jit_solution(4093856257660729635)
XLA Ops:
  0.6 100.8 %shard_map.68 = (bf16[256,512]{1,0:T(8,128)(2,1)}, f32[9,64,512]{2,1,0:T(8,128)}) custom-call(s32[2,32]{1,0:T(2,128)} %bitcast.16, s32[2,32]{1,0:T(2,128)} %bitcast.17, bf16[256,512]{1,0:T(8,128)(2,1)} %bitcast.13, bf16[256,512]{1,0:T(8,128)(2,1)} %bitcast.14, bf16[9,64,512]{2,1,0:T(8,128)(2,1)} %bitcast.12), custom_call_target="tpu_custom_call" | custom-call | tf_op jit(solution)/shard_map/pallas_call | solution.py:279
  101.4 1.7 %copy.9 = bf16[1,32,8,512]{3,2,1,0:T(8,128)(2,1)} copy(bf16[1,32,8,512]{3,2,1,0:T(8,128)(2,1)} %bitcast.15) | data formatting | bytes 524288
  103.1 2.4 %copy.10 = f32[1,1,9,64,512]{4,3,2,1,0:T(8,128)} copy(f32[1,1,9,64,512]{4,3,2,1,0:T(8,128)} %bitcast.11) | data formatting | bytes 2359296

commit v2 on v1

--- a/solution.py
+++ b/solution.py
@@ -90,7 +90,7 @@
         iota((block, tiles * CELLS), 0) % CELLS == iota((block, tiles * CELLS), 1) % CELLS
     )
 
-    def pack_x(k, carry):
+    def pack_x(k):
         row = iota((block, tiles), 0)
         step_x = row // ROWS
         step_z = (step_x + k) % side
@@ -109,9 +109,8 @@
         choose[rows, :] = chosen
         packed = dot(chosen, x_ref[...]).astype(jnp.bfloat16)
         px[pl.ds(k * side, side)] = packed.reshape(side, ROWS, channels)
-        return carry
-
-    lax.fori_loop(0, side, pack_x, 0)
+
+    pack_x(0)
 
     pl.semaphore_wait(barrier, experts + 2)
 
@@ -135,8 +134,14 @@
         send(px, xr, o, 0, x_sem, ahead(o))
         return carry
 
+    def dispatch_x(k, carry):
+        pack_x(k)
+        lax.fori_loop(k * side, (k + 1) * side, send_x, 0)
+        return carry
+
     keep(px, xr, x_sem)
-    lax.fori_loop(1, experts, send_x, 0)
+    lax.fori_loop(1, side, send_x, 0)
+    lax.fori_loop(1, side, dispatch_x, 0)
 
     same_group = iota((HALF, HALF), 0) // gw == iota((HALF, HALF), 1) // gw
     for half in range(halves):
@@ -149,20 +154,24 @@
 
     relay.wait_recv()
 
-    def pack_d(k, carry):
+    def pack_d(k):
         rows = pl.ds(pl.multiple_of(k * block, block), block)
         packed = (dot(choose[rows, :], dy[...]) * gates[rows, :]).astype(jnp.bfloat16)
         pd[pl.ds(k * side, side)] = packed.reshape(side, ROWS, channels)
-        return carry
-
-    lax.fori_loop(0, side, pack_d, 0)
 
     def send_d(o, carry):
         send(pd, dr, o, 1, d_sem, ahead(o))
         return carry
 
+    def dispatch_d(k, carry):
+        pack_d(k)
+        lax.fori_loop(k * side, (k + 1) * side, send_d, 0)
+        return carry
+
+    pack_d(0)
     keep(pd, dr, d_sem)
-    lax.fori_loop(1, experts, send_d, 0)
+    lax.fori_loop(1, side, send_d, 0)
+    lax.fori_loop(1, side, dispatch_d, 0)
 
     eye = (
         iota((tiles * CELLS, tiles * CELLS), 0) == iota((tiles * CELLS, tiles * CELLS), 1)
@@ -243,6 +252,10 @@
             dwm[tap, :, half * HALF:(half + 1) * HALF] = picked
         swap(tap).start()
 
+    for tap in range(9):
+        swap(tap).wait_recv()
+        dw_ref[tap] = (dwm[tap] + dwo[tap]) * (1.0 / tiles)
+
     acc[...] = dy[...].astype(jnp.float32)
 
     def combine(k, carry):
@@ -254,10 +267,6 @@
 
     lax.fori_loop(0, side, combine, 0)
     dx_ref[...] = acc[...].astype(jnp.bfloat16)
-
-    for tap in range(9):
-        swap(tap).wait_recv()
-        dw_ref[tap] = (dwm[tap] + dwo[tap]) * (1.0 / tiles)
 
     relay.wait_send()
     for tap in range(9):
@@ -299,7 +308,7 @@
             dma((3,)), dma((2,)), dma((side,)), dma((side,)), dma((side,)), dma((9,)), dma((9,)),
         ],
         compiler_params=pltpu.CompilerParams(
-            collective_id=0, has_side_effects=True, vmem_limit_bytes=56 * 1024 * 1024
+            collective_id=0, has_side_effects=True, vmem_limit_bytes=32 * 1024 * 1024
         ),
     )(
         routes[0].T,

time: 106 us -> 115 us (1.085)
  the two profiles are of different devices: /device:TPU:44 before, /device:TPU:77 now
where the time goes in v2:
time: 115 us
  Pallas kernels  108 us (94%)
  local copies, waits for them, and re-layouts  6.03 us (5%)
    pallas_call x1, Pallas kernels, body(): pl.pallas_call(functools.partial(kernel, side, segments), out_shape=(jax....  108 us
    unnamed x12, local copies, waits for them, and re-layouts  6.03 us

profile of v2, /device:TPU:77, one launch (start us, length us, event | category | flops | bytes accessed | tf_op | source)
XLA Modules:
  0.0 115.0 jit_solution(4147459688627310112)
XLA Ops:
  0.6 0.0 copy-start
  0.6 1.1 copy-done
  1.7 0.0 copy-start.1
  1.7 0.9 copy-done.1
  2.6 0.0 copy-start.2
  2.6 0.9 copy-done.2
  3.6 0.0 copy-start.3
  3.6 0.7 copy-done.3
  4.3 0.0 copy-start.4
  4.3 0.7 copy-done.4
  5.0 108.4 %shard_map.68 = (bf16[256,512]{1,0:T(8,128)(2,1)S(1)}, f32[9,64,512]{2,1,0:T(8,128)S(1)}) custom-call(s32[2,32]{1,0:T(2,128)S(1)} %bitcast.16, s32[2,32]{1,0:T(2,128)S(1)} %bitcast.17, bf16[256,512]{1,0:T(8,128)(2,1)S(1)} %bitcast.13, bf16[256,512]{1,0:T(8,128)(2,1)S(1)} %bitcast.14, bf16[9,64,512]{2,1,0:T(8,128)(2,1)S(1)} %bitcast.12), custom_call_target="tpu_custom_call" | custom-call | tf_op jit(solution)/shard_map/pallas_call | solution.py:288
  113.3 0.7 copy.9
  114.0 1.0 copy.10
Async XLA Ops:
  0.6 1.1 copy-start
  1.7 0.9 copy-start.1
  2.6 0.9 copy-start.2
  3.6 0.7 copy-start.3
  4.3 0.7 copy-start.4

commit v3 on v1

--- a/solution.py
+++ b/solution.py
@@ -36,7 +36,7 @@
     routes_ref, codes_ref, x_ref, up_ref, w_ref,
     dx_ref, dw_ref,
     px, pd, an, xr, dr, ar, dy, choose, chooset, gates, dall, bd, xt, acc, dwm, dwo,
-    send_sem, relay_sem, x_sem, d_sem, a_sem, dw_send, dw_sem,
+    send_sem, relay_sem, x_sem, d_sem, a_sem, dw_send, dw_sem, dw_out,
 ):
     experts = side * side
     tiles = routes_ref.shape[1]
@@ -243,6 +243,14 @@
             dwm[tap, :, half * HALF:(half + 1) * HALF] = picked
         swap(tap).start()
 
+    def stored(tap):
+        return pltpu.make_async_copy(dwm.at[tap], dw_ref.at[tap], dw_out.at[tap])
+
+    for tap in range(9):
+        swap(tap).wait()
+        dwm[tap] = (dwm[tap] + dwo[tap]) * (1.0 / tiles)
+        stored(tap).start()
+
     acc[...] = dy[...].astype(jnp.float32)
 
     def combine(k, carry):
@@ -255,16 +263,47 @@
     lax.fori_loop(0, side, combine, 0)
     dx_ref[...] = acc[...].astype(jnp.bfloat16)
 
-    for tap in range(9):
-        swap(tap).wait_recv()
-        dw_ref[tap] = (dwm[tap] + dwo[tap]) * (1.0 / tiles)
-
     relay.wait_send()
     for tap in range(9):
-        swap(tap).wait_send()
+        stored(tap).wait()
     for kind, source in enumerate((px, pd, an)):
         sent = source.at[pl.ds(1, experts - 1)]
         pltpu.make_async_copy(sent, sent, send_sem.at[kind]).wait()
+
+
+PIECES = 3
+
+
+def hand_over_kernel(dx_in, dw_in, dx_out, dw_out, dx_held, dw_held, loads, stores):
+    taps = dw_in.shape[0] // PIECES
+    parts = [(dw_in.at[pl.ds(i * taps, taps)], dw_held.at[pl.ds(i * taps, taps)],
+              dw_out.at[pl.ds(i * taps, taps)]) for i in range(PIECES)]
+    parts.append((dx_in, dx_held, dx_out))
+    loading = [pltpu.make_async_copy(a, b, loads.at[i]) for i, (a, b, _) in enumerate(parts)]
+    storing = [pltpu.make_async_copy(b, c, stores.at[i]) for i, (_, b, c) in enumerate(parts)]
+    for load in loading:
+        load.start()
+    for load, store in zip(loading, storing):
+        load.wait()
+        store.start()
+    for store in storing:
+        store.wait()
+
+
+def hand_over(input_grad, weight_grad):
+    hbm = pl.BlockSpec(memory_space=pltpu.HBM)
+    arrays = (input_grad, weight_grad)
+    return pl.pallas_call(
+        hand_over_kernel,
+        out_shape=tuple(jax.ShapeDtypeStruct(a.shape, a.dtype) for a in arrays),
+        in_specs=[hbm, hbm],
+        out_specs=(hbm, hbm),
+        scratch_shapes=[pltpu.VMEM(a.shape, a.dtype) for a in arrays]
+        + [pltpu.SemaphoreType.DMA((PIECES + 1,))] * 2,
+        compiler_params=pltpu.CompilerParams(
+            has_side_effects=True, vmem_limit_bytes=56 * 1024 * 1024
+        ),
+    )(*arrays)
 
 
 def body(side, segments, activations, upstream, routes, gate_codes, weights):
@@ -283,7 +322,7 @@
             jax.ShapeDtypeStruct((taps, gw, channels), f32),
         ),
         in_specs=[vmem] * 5,
-        out_specs=(vmem, vmem),
+        out_specs=(vmem, pl.BlockSpec(memory_space=pltpu.HBM)),
         scratch_shapes=[pltpu.VMEM(message, bf16)] * 6
         + [
             pltpu.VMEM((tiles * cells, channels), bf16),
@@ -296,7 +335,7 @@
             pltpu.VMEM((tiles * cells, channels), f32),
             pltpu.VMEM((taps, gw, channels), f32),
             pltpu.VMEM((taps, gw, channels), f32),
-            dma((3,)), dma((2,)), dma((side,)), dma((side,)), dma((side,)), dma((9,)), dma((9,)),
+            dma((3,)), dma((2,)), dma((side,)), dma((side,)), dma((side,)), dma((9,)), dma((9,)), dma((9,)),
         ],
         compiler_params=pltpu.CompilerParams(
             collective_id=0, has_side_effects=True, vmem_limit_bytes=56 * 1024 * 1024
@@ -308,6 +347,7 @@
         upstream.reshape(tiles * cells, channels),
         weights[0, 0],
     )
+    input_grad, weight_grad = hand_over(input_grad, weight_grad)
     return (
         input_grad.reshape(1, tiles, cells, channels),
         weight_grad.reshape(1, 1, taps, gw, channels),

time: 106 us -> 105 us (level)
  local copies, waits for them, and re-layouts: 4.03 us -> 0 us
  Pallas kernels: 101 us -> 103 us
    unnamed x2 -> x0, local copies, waits for them, and re-layouts: 4.03 us -> none
    pallas_call x0 -> x1, Pallas kernels: none -> 2.16 us  [hand_over(): pl.pallas_call(hand_over_kernel, out_shape=tuple((jax.ShapeDtypeStruct(a....]
where the time goes in v3:
time: 105 us; the launch traced here: 104 us
  Pallas kernels  103 us (98%)
    pallas_call x1, Pallas kernels, body(): pl.pallas_call(functools.partial(kernel, side, segments), out_shape=(jax....  101 us
    pallas_call x1, Pallas kernels, hand_over(): pl.pallas_call(hand_over_kernel, out_shape=tuple((jax.ShapeDtypeStruct(a....  2.16 us

profile of v3, /device:TPU:44, one launch (start us, length us, event | category | flops | bytes accessed | tf_op | source)
XLA Modules:
  0.0 104.1 jit_solution(5643473705644991885)
XLA Ops:
  0.6 101.3 %shard_map.68 = (bf16[256,512]{1,0:T(8,128)(2,1)}, f32[9,64,512]{2,1,0:T(8,128)}) custom-call(s32[2,32]{1,0:T(2,128)} %bitcast.14, s32[2,32]{1,0:T(2,128)} %bitcast.15, bf16[256,512]{1,0:T(8,128)(2,1)} %bitcast.12, bf16[256,512]{1,0:T(8,128)(2,1)} %bitcast.13, bf16[9,64,512]{2,1,0:T(8,128)(2,1)} %bitcast.11), custom_call_target="tpu_custom_call" | custom-call | tf_op jit(solution)/shard_map/pallas_call | solution.py:318
  102.0 2.2 %shard_map.69 = (bf16[256,512]{1,0:T(8,128)(2,1)}, f32[9,64,512]{2,1,0:T(8,128)}) custom-call(bf16[256,512]{1,0:T(8,128)(2,1)} %get-tuple-element.6.dx_in, f32[9,64,512]{2,1,0:T(8,128)} %get-tuple-element.7.dw_in), custom_call_target="tpu_custom_call" | custom-call | tf_op jit(solution)/shard_map/pallas_call | solution.py:296
